TPU v7x, 256 devices: a whole 4x4x8 slice. The times are simulated.
256 devices in a mesh: dp: 128 (over z, y, x), sub: 2 (over core).
Axes of the slice: x: 4, y: 4, z: 8, core: 2. Of those that a mesh axis runs over, the one named last changes fastest.
Arguments:
- grads: bfloat16 [128, 2, 2048, 512], P('dp', None, 'sub'), may hold values from -84 to 84
- errors: bfloat16 [128, 2, 2048, 512], P('dp', None, 'sub'), may hold values from -3 to 3
- vec_grads: float32 [128, 2, 2048], P('dp', None, 'sub'), may hold values from -24 to 24
- gains: float32 [2, 2048], P(None, 'sub'), may hold values from 0.5 to 1.5
- q_start: float32 [2, 512, 32], replicated, may hold values from -0.25 to 0.25
- owner: int32 [256], replicated, may hold values from 0 to 127, as said below
- momentum: float32 [512, 16, 512], P('dp', None, 'sub'), may hold values from -3 to 3
- master: float32 [512, 16, 512], P('dp', None, 'sub'), may hold values from -5 to 5
Outputs:
- errors_out: bfloat16 [128, 2, 2048, 512], P('dp', None, 'sub')
- new_gains: float32 [2, 2048], P(None, 'sub')
- new_momentum: float32 [512, 16, 512], P('dp', None, 'sub')
- new_master: float32 [512, 16, 512], P('dp', None, 'sub')
- weights: bfloat16 [2, 2048, 512], P(None, None, 'sub')
Inputs may be any that keep to these rules, and one draw needn't show every extreme that they name: `owner`: each dp index owns at most 4 blocks and some index owns exactly 4; momentum and master in empty slots are not used.
All inputs are finite; a program needn't handle non-finite values.
Results may differ from a plain program's by a relative error of at most 0.005.
Values may be sent and summed in bfloat16 or wider, within the bound.
A program may use at most 128 MiB of HBM per device.

v0:
```python
import jax
import jax.numpy as jnp
from jax import lax
from jax.sharding import PartitionSpec as P

ROUNDS = 2


HIGH = lax.Precision.HIGHEST
momentum_decay = 0.9
step_rate = 0.5
vector_rate = 1.0


def solve_basis(left, gram):
    lower = jnp.linalg.cholesky(gram)
    return lax.linalg.triangular_solve(lower, left, left_side=False, lower=True, transpose_a=True)


def body(grads, errors, vec_grads, gains, q_start, owner, momentum, master):
    replicas = lax.axis_size("dp")
    slots = momentum.shape[0]
    rows_block = momentum.shape[1]
    half_cols = momentum.shape[2]
    blocks = owner.shape[0]
    mixed = grads[0].astype(jnp.float32) + errors[0].astype(jnp.float32)
    mats = mixed.shape[0]
    vec_total = lax.psum(vec_grads[0], "dp")
    new_gains = gains - vector_rate * (vec_total / replicas)
    right = q_start
    for step_index in range(ROUNDS):
        local_left = jnp.einsum("mdk,mkr->mdr", mixed, right, precision=HIGH)
        left = lax.psum(local_left, "dp") / replicas
        gram = lax.psum(jnp.einsum("mdr,mds->mrs", left, left, precision=HIGH), "sub")
        basis = solve_basis(left, gram)
        local_right = jnp.einsum("mdk,mdr->mkr", mixed, basis, precision=HIGH)
        right = lax.psum(local_right, ("dp", "sub")) / replicas
    approx_local = jnp.einsum("mdr,mkr->mdk", basis, right, precision=HIGH)
    errors_out = (mixed - approx_local).astype(jnp.bfloat16)[None]
    basis_full = lax.all_gather(basis.astype(jnp.bfloat16), "sub", axis=1, tiled=True).astype(
        basis.dtype
    )
    right_half = lax.dynamic_slice_in_dim(right, lax.axis_index("sub") * half_cols, half_cols, 1)
    approx_half = jnp.einsum("mdr,mkr->mdk", basis_full, right_half, precision=HIGH)
    full_rows = basis_full.shape[1]
    approx_blocks = approx_half.reshape(blocks, rows_block, half_cols)
    index = jnp.arange(blocks, dtype=jnp.int32)
    same = owner[:, None] == owner[None, :]
    earlier = index[None, :] < index[:, None]
    rank = jnp.sum((same & earlier).astype(jnp.int32), axis=1)
    pos = owner * slots + rank
    mine = (owner[None, :] == lax.axis_index("dp")) & (
        rank[None, :] == jnp.arange(slots, dtype=jnp.int32)[:, None]
    )
    mine_int = mine.astype(jnp.int32)
    local_block = jnp.sum(mine_int * index[None, :], axis=1)
    valid = jnp.sum(mine_int, axis=1).astype(jnp.float32)[:, None, None]
    approx_slots = approx_blocks[local_block] * valid
    new_momentum = (momentum_decay * momentum + approx_slots) * valid
    new_master = (master - step_rate * new_momentum) * valid
    gathered = lax.all_gather(new_master.astype(jnp.bfloat16), "dp", axis=0, tiled=True)
    weights = gathered[pos].reshape(mats, full_rows, half_cols)
    return (errors_out, new_gains, new_momentum, new_master, weights)


def solution(mesh):
    placed = (
        P("dp", None, "sub", None),
        P("dp", None, "sub", None),
        P("dp", None, "sub"),
        P(None, "sub"),
        P(),
        P(),
        P("dp", None, "sub"),
        P("dp", None, "sub"),
    )
    return jax.shard_map(
        body,
        mesh=mesh,
        in_specs=placed,
        out_specs=(
            P("dp", None, "sub", None),
            P(None, "sub"),
            P("dp", None, "sub"),
            P("dp", None, "sub"),
            P(None, None, "sub"),
        ),
        check_vma=False,
    )
```

profile of v0, /device:TPU:2, one launch (start us, length us, event | category | flops | bytes accessed | tf_op | source)
XLA Modules:
  0.0 1345.0 jit_solution(2822538106656851169)
XLA Ops:
  7.2 0.0 copy-start
  7.2 0.0 copy-start.1
  7.2 0.0 copy-start.5
  7.2 0.0 all-reduce.5.cloned.1.call-start
  7.2 0.8 copy-done
  8.1 7.2 fusion.6
  15.3 0.0 all-reduce.5.cloned.1.call-update
  15.3 0.0 all-reduce.7.cloned.1.call-start
  15.4 0.0 copy-done.5
  15.4 0.2 convert_reduce_fusion
  15.6 215.6 %all-reduce.5.cloned.1.call-done = f32[2,1024,32]{1,2,0:T(8,128)} async-done(((f32[2,1024,32]{1,2,0:T(8,128)}), f32[2,1024,32]{1,2,0:T(8,128)}) %all-reduce.5.cloned.1.call-update) | async-done | bytes 262160 | tf_op jit(solution)/shard_map/psum | solution.py:33
  231.1 1.4 fusion.15
  232.5 3.4 psum.50
  236.0 0.1 copy.30
  236.0 5.9 custom-call.8
  241.9 0.1 compare_reduce_fusion.1
  242.1 0.1 select_bitcast_fusion.1
  242.1 4.9 custom-call.9
  247.1 1.4 convolution_bitcast_fusion.1
  248.4 0.0 copy-done.1
  248.5 5.2 fusion.4
  253.7 0.0 all-reduce.7.cloned.1.call-update
  253.7 0.0 all-reduce.9.cloned.1.call-start
  253.8 0.1 convert_reduce_fusion.1
  253.9 239.2 %all-reduce.7.cloned.1.call-done = f32[2,512,32]{1,2,0:T(8,128)} async-done(((f32[2,512,32]{1,2,0:T(8,128)}), f32[2,512,32]{1,2,0:T(8,128)}) %all-reduce.7.cloned.1.call-update) | async-done | bytes 131088 | tf_op jit(solution)/shard_map/psum | solution.py:37
  493.1 6.6 fusion.2
  499.7 0.0 all-reduce.9.cloned.1.call-update
  499.7 0.0 all-reduce.11.cloned.1.call-start
  499.8 209.7 %all-reduce.9.cloned.1.call-done = f32[2,1024,32]{1,2,0:T(8,128)} async-done(((f32[2,1024,32]{1,2,0:T(8,128)}), f32[2,1024,32]{1,2,0:T(8,128)}) %all-reduce.9.cloned.1.call-update) | async-done | bytes 262160 | tf_op jit(solution)/shard_map/psum | solution.py:33
  709.5 1.4 fusion.12
  710.9 3.6 psum.53
  714.5 0.1 copy.33
  714.6 5.9 custom-call.10
  720.5 0.1 compare_reduce_fusion
  720.6 0.1 select_bitcast_fusion
  720.7 4.9 custom-call.11
  725.6 1.4 fusion.38
  727.0 0.0 copy-start.3
  727.0 0.0 copy-start.4
  727.0 0.0 copy-start.7
  727.0 0.0 copy-start.6
  727.0 5.3 fusion
  732.3 0.0 all-reduce.11.cloned.1.call-update
  732.3 0.0 all-gather.2.cloned.1.call-start
  732.4 2.0 all_gather.6
  734.4 237.4 %all-reduce.11.cloned.1.call-done = f32[2,512,32]{1,2,0:T(8,128)} async-done(((f32[2,512,32]{1,2,0:T(8,128)}), f32[2,512,32]{1,2,0:T(8,128)}) %all-reduce.11.cloned.1.call-update) | async-done | bytes 131088 | tf_op jit(solution)/shard_map/psum | solution.py:37
  971.8 0.0 copy-start.2
  971.8 1.0 broadcast_multiply_fusion
  972.8 3.8 fusion.22
  976.5 2.7 gather_fusion
  979.3 0.0 copy-done.3
  979.3 0.0 copy-done.4
  979.3 0.7 fusion.37
  980.0 0.0 all-gather.2.cloned.1.call-update
  980.1 0.0 copy-done.7
  980.1 347.4 %psum.55 = f32[2,1024]{1,0:T(2,128)S(1)} all-reduce(f32[2,1024]{1,0:T(2,128)S(1)} %bitcast.54), channel_id=1, replica_groups=mesh['dp'=128,'sub'=2] {'dp'}, use_global_device_ids=true, to_apply=%region_8.11 | all-reduce | flops 2048 | bytes 16384 | tf_op jit(solution)/shard_map/psum | solution.py:28
  1327.5 0.0 copy-done.6
  1327.5 0.6 multiply_subtract_fusion
  1328.1 0.0 copy-done.2
  1328.1 6.1 fusion.9
  1334.2 0.0 all-gather.2.cloned.1.call-done
  1334.2 4.3 gather_fusion.1
  (12 shorter events, 0.1 us)
Async XLA Ops:
  7.2 0.9 copy-start
  7.2 241.3 %copy-start.1 = (bf16[1,2,1024,512]{3,2,1,0:T(8,128)(2,1)S(1)}, bf16[1,2,1024,512]{3,2,1,0:T(8,128)(2,1)}, u32[]{:S(2)}) copy-start(bf16[1,2,1024,512]{3,2,1,0:T(8,128)(2,1)} %param.12) | copy-start | bytes 6291460
  7.2 8.2 copy-start.5
  7.2 223.9 %all-reduce.5.cloned.1.call-start = ((), (), s32[]{:S(2)}) async-start(), calls=%async_computation | async-start | bytes 524288 | tf_op jit(solution)/shard_map/psum | solution.py:33
  15.3 477.8 %all-reduce.7.cloned.1.call-start = ((), (), s32[]{:S(2)}) async-start(), calls=%async_computation.1 | async-start | bytes 262144 | tf_op jit(solution)/shard_map/psum | solution.py:37
  253.7 455.8 %all-reduce.9.cloned.1.call-start = ((), (), s32[]{:S(2)}) async-start(), calls=%async_computation.2 | async-start | bytes 524288 | tf_op jit(solution)/shard_map/psum | solution.py:33
  499.7 472.0 %all-reduce.11.cloned.1.call-start = ((), (), s32[]{:S(2)}) async-start(), calls=%async_computation.3 | async-start | bytes 262144 | tf_op jit(solution)/shard_map/psum | solution.py:37
  727.0 252.3 %copy-start.3 = (f32[4,16,256]{2,1,0:T(8,128)S(1)}, f32[4,16,256]{2,1,0:T(8,128)}, u32[]{:S(2)}) copy-start(f32[4,16,256]{2,1,0:T(8,128)} %param.18) | copy-start | bytes 196612
  727.0 252.3 %copy-start.4 = (f32[4,16,256]{2,1,0:T(8,128)S(1)}, f32[4,16,256]{2,1,0:T(8,128)}, u32[]{:S(2)}) copy-start(f32[4,16,256]{2,1,0:T(8,128)} %param.17) | copy-start | bytes 196612
  727.0 253.1 %copy-start.7 = (f32[1,2,1024]{2,1,0:T(2,128)S(1)}, f32[1,2,1024]{2,1,0:T(2,128)}, u32[]{:S(2)}) copy-start(f32[1,2,1024]{2,1,0:T(2,128)} %param.13) | copy-start | bytes 24580
  727.0 600.5 %copy-start.6 = (f32[2,1024]{1,0:T(2,128)S(1)}, f32[2,1024]{1,0:T(2,128)}, u32[]{:S(2)}) copy-start(f32[2,1024]{1,0:T(2,128)} %param.14) | copy-start | bytes 24580
  732.3 601.9 %all-gather.2.cloned.1.call-start = ((), (), s32[]{:S(2)}) async-start(), calls=%async_computation.4 | async-start | bytes 4227072 | tf_op jit(solution)/shard_map/all_gather | solution.py:61
  971.8 356.3 %copy-start.2 = (f32[2,512,32]{1,2,0:T(8,128)S(1)}, f32[2,512,32]{1,2,0:T(8,128)}, u32[]{:S(2)}) copy-start(f32[2,512,32]{1,2,0:T(8,128)} %all-reduce.11.cloned.1.call-done) | copy-start | bytes 393220
Sparse Core Ops, SparseCore 0:
  15.4 215.6 all-reduce.4
  253.8 239.2 all-reduce.6
  500.0 209.4 all-reduce.8
  732.5 239.2 all-reduce.10
  980.2 113.5 all-gather.1
where the time goes:
time: 1350 us
  waiting for transfers between devices  902 us (67%)
  blocking collectives  356 us (26%)
  matrix products  39.8 us (3%)
  other arithmetic  24.7 us (2%)
  between operations  14 us (1%)
    psum x2, waiting for transfers between devices, body(): right = lax.psum(local_right, ('dp', 'sub')) / replicas  477 us
    psum x2, waiting for transfers between devices, body(): left = lax.psum(local_left, 'dp') / replicas  425 us
    psum x1, blocking collectives, body(): vec_total = lax.psum(vec_grads[0], 'dp')  347 us
  transfers between devices with their start and end apart: 5, of which 4 were waited for; matrix products, arithmetic and copies ran while one was open for 1% of the time, Pallas kernels for 0%

commit v1 on v0

v1 whole, which is shorter than its diff:
```python
import functools

import jax
import jax.numpy as jnp
from jax import lax
from jax.experimental import pallas as pl
from jax.experimental.pallas import tpu as pltpu
from jax.sharding import PartitionSpec as P

MESH = pl.DeviceIdType.MESH
F32 = jnp.float32
BF16 = jnp.bfloat16
HIGH = lax.Precision.HIGHEST

ROUNDS = 2
MOMENTUM_DECAY = 0.9
STEP_RATE = 0.5
VECTOR_RATE = 1.0

LANES = 128
TILE = 8
BLOCK = 16
UNITS = 8

ORDERS = (((2, 1, 0), 0, 3), ((1, 0, 2), 3, 3), ((0, 2, 1), 6, 2))


def torus(dp):
    return {128: (8, 4, 4), 16: (4, 2, 2), 8: (2, 2, 2)}[dp]


def split3(value):
    high = value.astype(BF16)
    rest = value - high.astype(F32)
    middle = rest.astype(BF16)
    low = (rest - middle.astype(F32)).astype(BF16)
    return high, middle, low


def nt(a, b):
    return lax.dot_general(a, b, (((1,), (1,)), ((), ())), preferred_element_type=F32)


def nn(a, b):
    return lax.dot_general(a, b, (((1,), (0,)), ((), ())), preferred_element_type=F32)


def chains(n):
    found = []
    for longer in (True, False):
        for direction in (1, -1):
            half = 0 if (direction == 1) == longer else 1
            hops = n // 2 if longer else n // 2 - 1
            if hops:
                found.append((direction, half, hops))
    return found


def hop_table(n):
    table = {}
    for number, (_, _, hops) in enumerate(chains(n)):
        for hop in range(1, hops + 1):
            table[number, hop] = len(table)
    return table


def inverse_factor(gram0, gram1):
    rank = gram0.shape[0]
    rows = lax.broadcasted_iota(jnp.int32, (rank, LANES), 0)
    lanes = lax.broadcasted_iota(jnp.int32, (rank, LANES), 1)
    eye = (lax.broadcasted_iota(jnp.int32, (rank, rank), 0) == lax.broadcasted_iota(jnp.int32, (rank, rank), 1)).astype(F32)
    table = jnp.concatenate([gram0, eye, gram1, eye], axis=1)
    first = lanes < 2 * rank
    pivots = jnp.ones((rank, LANES), F32)
    for k in range(rank):
        column = jnp.where(first, table[:, k : k + 1], table[:, 2 * rank + k : 2 * rank + k + 1])
        pivot = column[k : k + 1, :]
        pivots = jnp.where(rows == k, pivot, pivots)
        if k < rank - 1:
            scaled = table[k : k + 1, :] / pivot
            table = table - jnp.where(rows > k, column * scaled, 0.0)
    table = table * lax.rsqrt(pivots)
    return table[:, rank : 2 * rank], table[:, 3 * rank : 4 * rank]


class Exchange:
    def __init__(self, sizes):
        self.sizes = sizes
        dp = lax.axis_index("dp")
        nz, ny, nx = sizes
        self.me = (dp // (ny * nx), (dp // nx) % ny, dp % nx)
        self.sub = lax.axis_index("sub")
        self.sent = []

    def peer(self, axis, step):
        n = self.sizes[axis]
        place = list(self.me)
        place[axis] = lax.rem(place[axis] + (step % n), n)
        return (place[0] * self.sizes[1] + place[1]) * self.sizes[2] + place[2]

    def place(self, axis, step):
        n = self.sizes[axis]
        return lax.rem(self.me[axis] + (step % n), n)

    def copy(self, source, target, send, receive, peer, sub=None):
        made = pltpu.make_async_remote_copy(
            src_ref=source,
            dst_ref=target,
            send_sem=send,
            recv_sem=receive,
            device_id=(peer, self.sub if sub is None else sub),
            device_id_type=MESH,
        )
        made.start()
        self.sent.append(made)
        return made

    def cut(self, axes, units, half=None):
        index = []
        for axis in range(3):
            if axis in axes:
                index.append(axes[axis])
            elif half is not None and axis == half[0]:
                n = self.sizes[axis]
                index.append(pl.ds(half[1] * (n // 2), n // 2))
            else:
                index.append(slice(None))
        index.append(pl.ds(units[0], units[1]))
        return tuple(index)


def ring_scatter(ex, buffer, landing, send, receive, order, units):
    axis = order[0]
    n = ex.sizes[axis]
    halved = 1 if axis == 0 else 0
    table = hop_table(n)
    links = chains(n)
    copies = {}

    def start(number, hop):
        direction, half, hops = links[number]
        target = ex.place(axis, direction * (hops - hop + 1))
        at = table[number, hop]
        copies[number, hop] = ex.copy(
            buffer.at[ex.cut({axis: target}, units, (halved, half))],
            landing.at[at],
            send.at[at],
            receive.at[at],
            ex.peer(axis, direction),
        )

    for number in range(len(links)):
        start(number, 1)
    for hop in range(1, n // 2 + 1):
        for number, (direction, half, hops) in enumerate(links):
            if hop > hops:
                continue
            yield
            copies[number, hop].wait_recv()
            target = ex.place(axis, direction * (hops - hop))
            index = ex.cut({axis: target}, units, (halved, half))
            buffer[index] = buffer[index] + landing[table[number, hop]]
            if hop < hops:
                start(number, hop + 1)


def direct_scatter(ex, buffer, landing, send, receive, order, stage, units):
    axis = order[stage]
    n = ex.sizes[axis]
    fixed = {a: ex.me[a] for a in order[:stage]}
    copies = []
    for step in range(1, n):
        index = ex.cut({**fixed, axis: ex.place(axis, step)}, units)
        copies.append(
            ex.copy(buffer.at[index], landing.at[step - 1], send.at[step - 1], receive.at[step - 1], ex.peer(axis, step))
        )
    yield
    own = ex.cut({**fixed, axis: ex.me[axis]}, units)
    total = buffer[own]
    for step in range(1, n):
        copies[step - 1].wait_recv()
        total = total + landing[step - 1]
    buffer[own] = total


def direct_gather(ex, buffer, send, receive, order, stage, units):
    axis = order[stage]
    n = ex.sizes[axis]
    index = ex.cut({a: ex.me[a] for a in order[: stage + 1]}, units)
    copies = []
    for step in range(1, n):
        copies.append(
            ex.copy(buffer.at[index], buffer.at[index], send.at[step - 1], receive.at[step - 1], ex.peer(axis, step))
        )
    yield
    for made in copies:
        made.wait_recv()


def ring_gather(ex, buffer, send, receive, order, units):
    axis = order[0]
    n = ex.sizes[axis]
    halved = 1 if axis == 0 else 0
    table = hop_table(n)
    links = chains(n)
    copies = {}

    def start(number, hop):
        direction, half, _ = links[number]
        index = ex.cut({axis: ex.place(axis, -direction * (hop - 1))}, units, (halved, half))
        at = table[number, hop]
        copies[number, hop] = ex.copy(
            buffer.at[index], buffer.at[index], send.at[at], receive.at[at], ex.peer(axis, direction)
        )

    for number in range(len(links)):
        start(number, 1)
    for hop in range(1, n // 2 + 1):
        for number, (_, _, hops) in enumerate(links):
            if hop > hops:
                continue
            yield
            copies[number, hop].wait_recv()
            if hop < hops:
                start(number, hop + 1)


def vector_sum(ex, buffer, landing, send, receive):
    at = 0
    for axis in (2, 1, 0):
        n = ex.sizes[axis]
        copies = []
        stage = 2 - axis
        for step in range(1, n):
            slot = at + step - 1
            copies.append(
                ex.copy(buffer.at[stage], landing.at[slot], send.at[slot], receive.at[slot], ex.peer(axis, step))
            )
        yield
        total = buffer[stage]
        for step in range(1, n):
            copies[step - 1].wait_recv()
            total = total + landing[at + step - 1]
        buffer[stage + 1] = total
        at += n - 1


def chain(*parts):
    for part in parts:
        yield from part()


def interleave(*parts):
    live = list(parts)
    while live:
        for part in list(live):
            try:
                next(part)
            except StopIteration:
                live.remove(part)


def drain(part, steps):
    for _ in range(steps):
        try:
            next(part)
        except StopIteration:
            return


def share_kernel(sizes, *refs):
    refs = list(refs)
    take = lambda count: [refs.pop(0) for _ in range(count)]
    grads, errors, vec_grads, q_start, momentum, master = take(6)
    basis_out, right_out, vec_out, slots_out = take(4)
    raw_g, raw_e, load_sem, work, mean = take(5)
    high, low = take(2)
    vec_buf, vec_land, vec_send, vec_recv = take(4)
    left_t = take(1)[0]
    mine, theirs, core_send, core_recv = take(4)
    basis_mine, basis_theirs = take(2)
    slots_mine = take(1)[0]
    lands, sends, recvs = [], [], []
    for _ in ORDERS:
        lands.append(take(3))
        sends.append(take(9))
        recvs.append(take(9))

    nz, ny, nx = sizes
    ex = Exchange(sizes)
    rank = q_start.shape[2]
    cols = q_start.shape[1]
    groups = cols // LANES
    plane = ny * nx * BLOCK
    per_mat = nz // 2
    dp_count = nz * ny * nx

    barrier = pltpu.get_barrier_semaphore()
    peers = [(ex.peer(axis, step), ex.sub) for axis in range(3) for step in range(1, sizes[axis])]
    peers.append((lax.axis_index("dp"), 1 - ex.sub))
    for peer in peers:
        pl.semaphore_signal(barrier, inc=1, device_id=peer, device_id_type=MESH)

    loads = []
    for z in range(nz):
        rows = pl.ds((z % per_mat) * plane, plane)
        pair = []
        for number, (source, target) in enumerate(((grads, raw_g), (errors, raw_e))):
            made = pltpu.make_async_copy(source.at[0, z // per_mat, rows], target.at[z], load_sem.at[z, number])
            made.start()
            pair.append(made)
        loads.append(pair)

    slots = master[...] - (STEP_RATE * MOMENTUM_DECAY) * momentum[...]
    slots = slots.astype(BF16)
    for slot in range(slots.shape[0]):
        for group in range(2):
            slots_mine[2 * slot + group] = slots[slot, :, group * LANES : (group + 1) * LANES]
    vec_buf[0] = vec_grads[0]
    own_slots = pltpu.make_async_copy(slots_mine, slots_out.at[ex.me[0], ex.me[1], ex.me[2]], load_sem.at[0, 2])
    own_slots.start()

    for z in range(nz):
        for made in loads[z]:
            made.wait()
        mixed = raw_g[z].astype(F32) + raw_e[z].astype(F32)
        for group in range(groups):
            tiles = mixed[:, group * LANES : (group + 1) * LANES].reshape(ny, nx, 2, TILE, LANES)
            work[z, :, :, 2 * group : 2 * group + 2] = tiles
    own_slots.wait()

    pl.semaphore_wait(barrier, len(peers))

    def scatter(number):
        order, first, count = ORDERS[number]
        units = (first, count)
        land, send, recv = lands[number], sends[number], recvs[number]
        yield from ring_scatter(ex, work, land[0], send[0], recv[0], order, units)
        yield from direct_scatter(ex, work, land[1], send[1], recv[1], order, 1, units)
        yield from direct_scatter(ex, work, land[2], send[2], recv[2], order, 2, units)
        own = ex.cut({a: ex.me[a] for a in range(3)}, units)
        mean[own] = work[own]
        yield from direct_gather(ex, mean, send[3], recv[3], order, 2, units)
        yield from direct_gather(ex, mean, send[4], recv[4], order, 1, units)
        yield from ring_gather(ex, mean, send[5], recv[5], order, units)

    def spread(number):
        order, first, count = ORDERS[number]
        units = (first, count)
        send, recv = sends[number], recvs[number]
        yield from direct_gather(ex, slots_out, send[6], recv[6], order, 2, units)
        yield from direct_gather(ex, slots_out, send[7], recv[7], order, 1, units)
        yield from ring_gather(ex, slots_out, send[8], recv[8], order, units)

    interleave(*[scatter(number) for number in range(3)], vector_sum(ex, vec_buf, vec_land, vec_send, vec_recv))
    vec_out[...] = vec_buf[3]
    spreads = [spread(number) for number in range(3)]

    def advance(steps=1):
        for _ in range(steps):
            for part in spreads:
                drain(part, 1)

    advance()
    scale = 1.0 / dp_count
    for z in range(nz):
        for group in range(groups):
            tiles = mean[z, :, :, 2 * group : 2 * group + 2].reshape(plane, LANES) * scale
            top = tiles.astype(BF16)
            high[z, :, group * LANES : (group + 1) * LANES] = top
            low[z, :, group * LANES : (group + 1) * LANES] = (tiles - top.astype(F32)).astype(BF16)
    advance()

    right_t = [q_start[m].T for m in range(2)]
    for step_index in range(ROUNDS):
        for m in range(2):
            q_terms = split3(right_t[m])
            q_all = jnp.concatenate(q_terms, axis=0)
            q_two = jnp.concatenate(q_terms[:2], axis=0)
            gram = jnp.zeros((3 * rank, 3 * rank), F32)
            product = jnp.zeros((3 * rank, cols), F32)
            product_low = jnp.zeros((2 * rank, cols), F32)
            for part in range(per_mat):
                z = m * per_mat + part
                top, rest = high[z], low[z]
                wide = nt(q_all, top)
                narrow = nt(q_two, rest)
                left = wide[:rank] + (wide[rank : 2 * rank] + wide[2 * rank :] + (narrow[:rank] + narrow[rank:]))
                left_t[m, :, part * plane : (part + 1) * plane] = left
                p_terms = split3(left)
                p_all = jnp.concatenate(p_terms, axis=0)
                p_two = jnp.concatenate(p_terms[:2], axis=0)
                gram = gram + nt(p_all, p_all)
                product = product + nn(p_all, top)
                product_low = product_low + nn(p_two, rest)
            total = product[:rank] + (
                product[rank : 2 * rank] + product[2 * rank :] + (product_low[:rank] + product_low[rank:])
            )
            mine[step_index, m, :, :cols] = total
            gram_rows = gram[:rank] + (gram[rank : 2 * rank] + gram[2 * rank :])
            square = gram_rows[:, :rank] + (gram_rows[:, rank : 2 * rank] + gram_rows[:, 2 * rank :])
            mine[step_index, m, :, cols:] = jnp.concatenate([square] * (LANES // rank), axis=1)
        made = ex.copy(
            mine.at[step_index],
            theirs.at[step_index],
            core_send.at[step_index],
            core_recv.at[step_index],
            lax.axis_index("dp"),
            1 - ex.sub,
        )
        advance()
        made.wait_recv()
        both = [mine[step_index, m] + theirs[step_index, m] for m in range(2)]
        inverses = inverse_factor(*[both[m][:, cols : cols + rank] for m in range(2)])
        right_t = [
            lax.dot_general(
                inverses[m], both[m][:, :cols], (((1,), (0,)), ((), ())), precision=HIGH, preferred_element_type=F32
            )
            for m in range(2)
        ]
        advance()
    for m in range(2):
        right_out[m] = right_t[m]
        basis_mine[m] = lax.dot_general(
            inverses[m], left_t[m], (((1,), (0,)), ((), ())), precision=HIGH, preferred_element_type=F32
        )
    made = ex.copy(
        basis_mine, basis_theirs, core_send.at[ROUNDS], core_recv.at[ROUNDS], lax.axis_index("dp"), 1 - ex.sub
    )
    for part in spreads:
        drain(part, 64)
    basis_out[ex.sub] = basis_mine[...]
    made.wait_recv()
    basis_out[1 - ex.sub] = basis_theirs[...]
    for made in ex.sent:
        made.wait_send()


def share(sizes, grads, errors, vec_grads, q_start, momentum, master):
    nz, ny, nx = sizes
    mats, rows, cols = grads.shape[1:]
    rank = q_start.shape[2]
    plane = ny * nx * BLOCK
    vmem = pl.BlockSpec(memory_space=pltpu.VMEM)
    anywhere = pl.BlockSpec(memory_space=pl.ANY)
    dma = pltpu.SemaphoreType.DMA
    wires = sum(n - 1 for n in sizes)
    scratch = [
        pltpu.VMEM((nz, plane, cols), BF16),
        pltpu.VMEM((nz, plane, cols), BF16),
        dma((nz, 3)),
        pltpu.VMEM((nz, ny, nx, UNITS, TILE, LANES), F32),
        pltpu.VMEM((nz, ny, nx, UNITS, TILE, LANES), F32),
        pltpu.VMEM((nz, plane, cols), BF16),
        pltpu.VMEM((nz, plane, cols), BF16),
        pltpu.VMEM((4,) + vec_grads.shape[1:], F32),
        pltpu.VMEM((wires,) + vec_grads.shape[1:], F32),
        dma((wires,)),
        dma((wires,)),
        pltpu.VMEM((mats, rank, rows), F32),
        pltpu.VMEM((ROUNDS, mats, rank, cols + LANES), F32),
        pltpu.VMEM((ROUNDS, mats, rank, cols + LANES), F32),
        dma((ROUNDS + 1,)),
        dma((ROUNDS + 1,)),
        pltpu.VMEM((mats, rank, rows), F32),
        pltpu.VMEM((mats, rank, rows), F32),
        pltpu.VMEM((UNITS, BLOCK, LANES), BF16),
    ]
    for order, _, count in ORDERS:
        first, second, third = order
        halved = 1 if first == 0 else 0
        shape = [sizes[a] // 2 if a == halved else sizes[a] for a in range(3) if a != first]
        hops = len(hop_table(sizes[first]))
        tail = (count, TILE, LANES)
        scratch.append(pltpu.VMEM((hops, *shape, *tail), F32))
        scratch.append(pltpu.VMEM((sizes[second] - 1, sizes[third], *tail), F32))
        scratch.append(pltpu.VMEM((sizes[third] - 1, *tail), F32))
        counts = [hops, sizes[second] - 1, sizes[third] - 1]
        counts = counts + counts[::-1] + counts[::-1]
        for _ in range(2):
            scratch.extend(dma((n,)) for n in counts)
    return pl.pallas_call(
        functools.partial(share_kernel, sizes),
        out_shape=(
            jax.ShapeDtypeStruct((2, mats, rank, rows), F32),
            jax.ShapeDtypeStruct((mats, rank, cols), F32),
            jax.ShapeDtypeStruct(vec_grads.shape[1:], F32),
            jax.ShapeDtypeStruct((nz, ny, nx, UNITS, BLOCK, LANES), BF16),
        ),
        in_specs=[anywhere, anywhere, vmem, vmem, vmem, vmem],
        out_specs=(vmem, vmem, vmem, anywhere),
        scratch_shapes=scratch,
        compiler_params=pltpu.CompilerParams(
            collective_id=0, has_side_effects=True, vmem_limit_bytes=56 * 1024 * 1024
        ),
        name="share",
    )(grads, errors, vec_grads, q_start, momentum, master)


def finish_kernel(steps, table, grads, errors, basis, right, gathered, momentum, master, vec, gains, *rest):
    errors_out, new_gains, new_momentum, new_master, weights, approx = rest
    step = pl.program_id(0)
    sub = table[0]
    blocks = approx.shape[0]
    slots = momentum.shape[0]
    per_mat = steps // 2
    mat = step // per_mat
    part = lax.rem(step, per_mat)
    rows = grads.shape[2]
    half_cols = weights.shape[2]

    def cat(values, first):
        top, middle, low = split3(values)
        return jnp.concatenate([top, top, middle, low] if first else [top, middle, top, top], axis=0)

    def product(left_t, right_t):
        return lax.dot_general(cat(left_t, True), cat(right_t, False), (((0,), (0,)), ((), ())), preferred_element_type=F32)

    local = basis[sub, mat, :, pl.ds(pl.multiple_of(part * rows, rows), rows)]
    mixed = grads[0, 0].astype(F32) + errors[0, 0].astype(F32)
    errors_out[0, 0] = (mixed - product(local, right[mat])).astype(BF16)

    half = part // (per_mat // 2)
    inner = lax.rem(part, per_mat // 2)
    wide = basis[half, mat, :, pl.ds(pl.multiple_of(inner * 2 * rows, 2 * rows), 2 * rows)]
    columns = right[mat, :, pl.ds(pl.multiple_of(sub * half_cols, half_cols), half_cols)]
    per_step = 2 * rows // BLOCK
    approx[pl.ds(step * per_step, per_step)] = product(wide, columns).reshape(per_step, BLOCK, half_cols)

    for number in range(per_step):
        block = step * per_step + number
        at = table[1 + block]
        for group in range(half_cols // LANES):
            lanes = slice(group * LANES, (group + 1) * LANES)
            value = gathered[at, group].astype(F32) - STEP_RATE * approx[block, :, lanes]
            weights[0, number * BLOCK : (number + 1) * BLOCK, lanes] = value.astype(BF16)

    @pl.when(step == steps - 1)
    def _():
        new_gains[...] = gains[...] - vec[...]
        for slot in range(slots):
            valid = table[1 + blocks + slots + slot] > 0
            moved = MOMENTUM_DECAY * momentum[slot] + approx[table[1 + blocks + slot]]
            moved = jnp.where(valid, moved, 0.0)
            new_momentum[slot] = moved
            new_master[slot] = jnp.where(valid, master[slot] - STEP_RATE * moved, 0.0)


def finish(steps, table, grads, errors, basis, right, gathered, momentum, master, vec, gains):
    mats, rows, cols = grads.shape[1:]
    blocks = 2 * mats * rows // BLOCK
    half_cols = momentum.shape[2]
    per_mat = steps // 2
    chunk = rows // per_mat
    moving = lambda i, t: (0, i // per_mat, i % per_mat, 0)
    whole = lambda shape: pl.BlockSpec(shape, lambda i, t: (0,) * len(shape))
    return pl.pallas_call(
        functools.partial(finish_kernel, steps),
        grid_spec=pltpu.PrefetchScalarGridSpec(
            num_scalar_prefetch=1,
            grid=(steps,),
            in_specs=[
                pl.BlockSpec((1, 1, chunk, cols), moving),
                pl.BlockSpec((1, 1, chunk, cols), moving),
                whole(basis.shape),
                whole(right.shape),
                whole(gathered.shape),
                whole(momentum.shape),
                whole(master.shape),
                whole(vec.shape),
                whole(gains.shape),
            ],
            out_specs=[
                pl.BlockSpec((1, 1, chunk, cols), moving),
                whole(gains.shape),
                whole(momentum.shape),
                whole(master.shape),
                pl.BlockSpec((1, 2 * chunk, half_cols), lambda i, t: (i // per_mat, i % per_mat, 0)),
            ],
            scratch_shapes=[pltpu.VMEM((blocks, BLOCK, half_cols), F32)],
        ),
        out_shape=(
            jax.ShapeDtypeStruct(grads.shape, BF16),
            jax.ShapeDtypeStruct(gains.shape, F32),
            jax.ShapeDtypeStruct(momentum.shape, F32),
            jax.ShapeDtypeStruct(master.shape, F32),
            jax.ShapeDtypeStruct((mats, 2 * rows, half_cols), BF16),
        ),
        compiler_params=pltpu.CompilerParams(vmem_limit_bytes=56 * 1024 * 1024),
        name="finish",
    )(table, grads, errors, basis, right, gathered, momentum, master, vec, gains)


def body(grads, errors, vec_grads, gains, q_start, owner, momentum, master):
    replicas = lax.axis_size("dp")
    sizes = torus(replicas)
    slots = momentum.shape[0]
    blocks = owner.shape[0]
    index = jnp.arange(blocks, dtype=jnp.int32)
    same = owner[:, None] == owner[None, :]
    earlier = index[None, :] < index[:, None]
    rank = jnp.sum((same & earlier).astype(jnp.int32), axis=1)
    pos = owner * slots + rank
    mine = (owner[None, :] == lax.axis_index("dp")) & (rank[None, :] == jnp.arange(slots, dtype=jnp.int32)[:, None])
    mine = mine.astype(jnp.int32)
    local_block = jnp.sum(mine * index[None, :], axis=1)
    valid = jnp.sum(mine, axis=1)
    table = jnp.concatenate([lax.axis_index("sub").astype(jnp.int32)[None], pos, local_block, valid])
    basis, right, vec, gathered = share(sizes, grads, errors, vec_grads, q_start, momentum, master)
    gathered = gathered.reshape(replicas * slots, 2, BLOCK, LANES)
    vec = vec * (VECTOR_RATE / replicas)
    errors_out, new_gains, new_momentum, new_master, weights = finish(
        sizes[0], table, grads, errors, basis, right, gathered, momentum, master, vec, gains
    )
    return (errors_out, new_gains, new_momentum, new_master, weights)


def solution(mesh):
    placed = (
        P("dp", None, "sub", None),
        P("dp", None, "sub", None),
        P("dp", None, "sub"),
        P(None, "sub"),
        P(),
        P(),
        P("dp", None, "sub"),
        P("dp", None, "sub"),
    )
    return jax.shard_map(
        body,
        mesh=mesh,
        in_specs=placed,
        out_specs=(
            P("dp", None, "sub", None),
            P(None, "sub"),
            P("dp", None, "sub"),
            P("dp", None, "sub"),
            P(None, None, "sub"),
        ),
        check_vma=False,
    )
```

time: 1350 us -> 162 us (0.12)
  the two profiles are of different devices: /device:TPU:2 before, /device:TPU:1 now
where the time goes in v1:
time: 162 us; the launch traced here: 161 us
  Pallas kernels  154 us (95%)
  other arithmetic  4.43 us (3%)
  local copies, waits for them, and re-layouts  1.9 us (1%)
    pallas_call x1, Pallas kernels, share(): pl.pallas_call(functools.partial(share_kernel, sizes), out_shape=(jax.Sha...  145 us
    pallas_call x1, Pallas kernels, finish(): pl.pallas_call(functools.partial(finish_kernel, steps), grid_spec=pltpu.P...  9.91 us

profile of v1, /device:TPU:1, one launch (start us, length us, event | category | flops | bytes accessed | tf_op | source)
XLA Modules:
  0.0 161.4 jit_solution(16275188837175238422)
XLA Ops:
  0.6 0.7 broadcast_compare_fusion
  1.3 0.9 convert_reduce_fusion
  2.3 0.2 select_reduce_fusion
  2.4 0.7 multiply_add_fusion
  3.1 0.7 pad_add_fusion.table
  3.8 1.9 %copy.14.refs_3_ = f32[2,512,32]{2,1,0:T(8,128)} copy(f32[2,512,32]{1,2,0:T(8,128)} %param.12) | data formatting | bytes 262144 | tf_op args[4]
  5.7 144.5 %share.1 = (f32[2,2,32,1024]{3,2,1,0:T(8,128)}, f32[2,32,512]{2,1,0:T(8,128)}, f32[2,1024]{1,0:T(2,128)}, bf16[8,4,4,8,16,128]{5,4,3,2,1,0:T(8,128)(2,1)}) custom-call(bf16[1,2,1024,512]{3,2,1,0:T(8,128)(2,1)} %grads.1, bf16[1,2,1024,512]{3,2,1,0:T(8,128)(2,1)} %errors.1, f32[1,2,1024]{2,1,0:T(2,128)} %refs_2_.1, f32[2,512,32]{2,1,0:T(8,128)} %copy.14.refs_3_, ...), custom_call_target="tpu_custom_call" | custom-call | tf_op jit(solution)/shard_map/share/pallas_call | solution.py:482
  150.2 1.3 broadcast_multiply_fusion.vec
  151.5 9.9 %finish.1 = (bf16[1,2,1024,512]{3,2,1,0:T(8,128)(2,1)}, f32[2,1024]{1,0:T(2,128)}, f32[4,16,256]{2,1,0:T(8,128)}, f32[4,16,256]{2,1,0:T(8,128)}, bf16[2,2048,256]{2,1,0:T(8,128)(2,1)}) custom-call(s32[265]{0:T(512)} %pad_add_fusion.table, bf16[1,2,1024,512]{3,2,1,0:T(8,128)(2,1)} %grads.1, bf16[1,2,1024,512]{3,2,1,0:T(8,128)(2,1)} %errors.1, ...), custom_call_target="tpu_custom_call" | custom-call | tf_op jit(solution)/shard_map/finish/pallas_call | solution.py:557

commit v2 on v1

--- a/solution.py
+++ b/solution.py
@@ -18,11 +18,11 @@
 VECTOR_RATE = 1.0
 
 LANES = 128
-TILE = 8
 BLOCK = 16
 UNITS = 8
-
-ORDERS = (((2, 1, 0), 0, 3), ((1, 0, 2), 3, 3), ((0, 2, 1), 6, 2))
+PARTS = 4
+
+ORDERS = (((2, 1, 0), (0, 2), (0, 3)), ((1, 0, 2), (2, 1), (3, 3)), ((0, 2, 1), (3, 1), (6, 2)))
 
 
 def torus(dp):
@@ -129,7 +129,7 @@
         return tuple(index)
 
 
-def ring_scatter(ex, buffer, landing, send, receive, order, units):
+def ring_scatter(ex, buffer, wire, landing, send, receive, order, units):
     axis = order[0]
     n = ex.sizes[axis]
     halved = 1 if axis == 0 else 0
@@ -142,7 +142,7 @@
         target = ex.place(axis, direction * (hops - hop + 1))
         at = table[number, hop]
         copies[number, hop] = ex.copy(
-            buffer.at[ex.cut({axis: target}, units, (halved, half))],
+            wire.at[ex.cut({axis: target}, units, (halved, half))],
             landing.at[at],
             send.at[at],
             receive.at[at],
@@ -159,27 +159,31 @@
             copies[number, hop].wait_recv()
             target = ex.place(axis, direction * (hops - hop))
             index = ex.cut({axis: target}, units, (halved, half))
-            buffer[index] = buffer[index] + landing[table[number, hop]]
+            total = buffer[index] + landing[table[number, hop]].astype(F32)
             if hop < hops:
+                wire[index] = total.astype(BF16)
                 start(number, hop + 1)
-
-
-def direct_scatter(ex, buffer, landing, send, receive, order, stage, units):
+            else:
+                buffer[index] = total
+
+
+def direct_scatter(ex, buffer, wire, landing, send, receive, order, stage, units):
     axis = order[stage]
     n = ex.sizes[axis]
     fixed = {a: ex.me[a] for a in order[:stage]}
     copies = []
     for step in range(1, n):
         index = ex.cut({**fixed, axis: ex.place(axis, step)}, units)
+        wire[index] = buffer[index].astype(BF16)
         copies.append(
-            ex.copy(buffer.at[index], landing.at[step - 1], send.at[step - 1], receive.at[step - 1], ex.peer(axis, step))
+            ex.copy(wire.at[index], landing.at[step - 1], send.at[step - 1], receive.at[step - 1], ex.peer(axis, step))
         )
     yield
     own = ex.cut({**fixed, axis: ex.me[axis]}, units)
     total = buffer[own]
     for step in range(1, n):
         copies[step - 1].wait_recv()
-        total = total + landing[step - 1]
+        total = total + landing[step - 1].astype(F32)
     buffer[own] = total
 
 
@@ -273,8 +277,8 @@
     take = lambda count: [refs.pop(0) for _ in range(count)]
     grads, errors, vec_grads, q_start, momentum, master = take(6)
     basis_out, right_out, vec_out, slots_out = take(4)
-    raw_g, raw_e, load_sem, work, mean = take(5)
-    high, low = take(2)
+    raw_g, raw_e, load_sem, work, wire, mean = take(6)
+    high = take(1)[0]
     vec_buf, vec_land, vec_send, vec_recv = take(4)
     left_t = take(1)[0]
     mine, theirs, core_send, core_recv = take(4)
@@ -288,8 +292,8 @@
 
     nz, ny, nx = sizes
     ex = Exchange(sizes)
-    rank = q_start.shape[2]
-    cols = q_start.shape[1]
+    rank = q_start.shape[1]
+    cols = q_start.shape[2]
     groups = cols // LANES
     plane = ny * nx * BLOCK
     per_mat = nz // 2
@@ -325,77 +329,75 @@
             made.wait()
         mixed = raw_g[z].astype(F32) + raw_e[z].astype(F32)
         for group in range(groups):
-            tiles = mixed[:, group * LANES : (group + 1) * LANES].reshape(ny, nx, 2, TILE, LANES)
-            work[z, :, :, 2 * group : 2 * group + 2] = tiles
+            tiles = mixed[:, group * LANES : (group + 1) * LANES].reshape(ny, nx, BLOCK, LANES)
+            work[z, :, :, group] = tiles
+            wire[z, :, :, group] = tiles.astype(BF16)
     own_slots.wait()
 
     pl.semaphore_wait(barrier, len(peers))
 
+    scale = 1.0 / dp_count
+    gathered = [False] * len(ORDERS)
+
     def scatter(number):
-        order, first, count = ORDERS[number]
-        units = (first, count)
+        order, units, _ = ORDERS[number]
         land, send, recv = lands[number], sends[number], recvs[number]
-        yield from ring_scatter(ex, work, land[0], send[0], recv[0], order, units)
-        yield from direct_scatter(ex, work, land[1], send[1], recv[1], order, 1, units)
-        yield from direct_scatter(ex, work, land[2], send[2], recv[2], order, 2, units)
+        yield from ring_scatter(ex, work, wire, land[0], send[0], recv[0], order, units)
+        yield from direct_scatter(ex, work, wire, land[1], send[1], recv[1], order, 1, units)
+        yield from direct_scatter(ex, work, wire, land[2], send[2], recv[2], order, 2, units)
         own = ex.cut({a: ex.me[a] for a in range(3)}, units)
-        mean[own] = work[own]
+        mean[own] = (work[own] * scale).astype(BF16)
         yield from direct_gather(ex, mean, send[3], recv[3], order, 2, units)
         yield from direct_gather(ex, mean, send[4], recv[4], order, 1, units)
         yield from ring_gather(ex, mean, send[5], recv[5], order, units)
-
-    def spread(number):
-        order, first, count = ORDERS[number]
-        units = (first, count)
+        assert gathered[number]
+        next(spreads[number])
+
+    def early(number):
+        order, _, units = ORDERS[number]
         send, recv = sends[number], recvs[number]
         yield from direct_gather(ex, slots_out, send[6], recv[6], order, 2, units)
         yield from direct_gather(ex, slots_out, send[7], recv[7], order, 1, units)
-        yield from ring_gather(ex, slots_out, send[8], recv[8], order, units)
-
-    interleave(*[scatter(number) for number in range(3)], vector_sum(ex, vec_buf, vec_land, vec_send, vec_recv))
-    vec_out[...] = vec_buf[3]
+        gathered[number] = True
+
+    def spread(number):
+        order, _, units = ORDERS[number]
+        yield from ring_gather(ex, slots_out, sends[number][8], recvs[number][8], order, units)
+
     spreads = [spread(number) for number in range(3)]
-
-    def advance(steps=1):
-        for _ in range(steps):
-            for part in spreads:
-                drain(part, 1)
-
-    advance()
-    scale = 1.0 / dp_count
+    interleave(
+        *[scatter(number) for number in range(3)],
+        vector_sum(ex, vec_buf, vec_land, vec_send, vec_recv),
+        *[early(number) for number in range(3)],
+    )
+    vec_out[...] = vec_buf[3] * (VECTOR_RATE / dp_count)
+
+    def advance():
+        for part in spreads:
+            drain(part, 4)
+
     for z in range(nz):
         for group in range(groups):
-            tiles = mean[z, :, :, 2 * group : 2 * group + 2].reshape(plane, LANES) * scale
-            top = tiles.astype(BF16)
-            high[z, :, group * LANES : (group + 1) * LANES] = top
-            low[z, :, group * LANES : (group + 1) * LANES] = (tiles - top.astype(F32)).astype(BF16)
-    advance()
-
-    right_t = [q_start[m].T for m in range(2)]
+            high[z, :, group * LANES : (group + 1) * LANES] = mean[z, :, :, group].reshape(plane, LANES)
+
+    right_t = [q_start[m] for m in range(2)]
     for step_index in range(ROUNDS):
         for m in range(2):
             q_terms = split3(right_t[m])
             q_all = jnp.concatenate(q_terms, axis=0)
-            q_two = jnp.concatenate(q_terms[:2], axis=0)
             gram = jnp.zeros((3 * rank, 3 * rank), F32)
             product = jnp.zeros((3 * rank, cols), F32)
-            product_low = jnp.zeros((2 * rank, cols), F32)
             for part in range(per_mat):
                 z = m * per_mat + part
-                top, rest = high[z], low[z]
+                top = high[z]
                 wide = nt(q_all, top)
-                narrow = nt(q_two, rest)
-                left = wide[:rank] + (wide[rank : 2 * rank] + wide[2 * rank :] + (narrow[:rank] + narrow[rank:]))
+                left = wide[:rank] + (wide[rank : 2 * rank] + wide[2 * rank :])
                 left_t[m, :, part * plane : (part + 1) * plane] = left
                 p_terms = split3(left)
                 p_all = jnp.concatenate(p_terms, axis=0)
-                p_two = jnp.concatenate(p_terms[:2], axis=0)
                 gram = gram + nt(p_all, p_all)
                 product = product + nn(p_all, top)
-                product_low = product_low + nn(p_two, rest)
-            total = product[:rank] + (
-                product[rank : 2 * rank] + product[2 * rank :] + (product_low[:rank] + product_low[rank:])
-            )
+            total = product[:rank] + (product[rank : 2 * rank] + product[2 * rank :])
             mine[step_index, m, :, :cols] = total
             gram_rows = gram[:rank] + (gram[rank : 2 * rank] + gram[2 * rank :])
             square = gram_rows[:, :rank] + (gram_rows[:, rank : 2 * rank] + gram_rows[:, 2 * rank :])
@@ -439,7 +441,7 @@
 def share(sizes, grads, errors, vec_grads, q_start, momentum, master):
     nz, ny, nx = sizes
     mats, rows, cols = grads.shape[1:]
-    rank = q_start.shape[2]
+    rank = q_start.shape[1]
     plane = ny * nx * BLOCK
     vmem = pl.BlockSpec(memory_space=pltpu.VMEM)
     anywhere = pl.BlockSpec(memory_space=pl.ANY)
@@ -449,9 +451,9 @@
         pltpu.VMEM((nz, plane, cols), BF16),
         pltpu.VMEM((nz, plane, cols), BF16),
         dma((nz, 3)),
-        pltpu.VMEM((nz, ny, nx, UNITS, TILE, LANES), F32),
-        pltpu.VMEM((nz, ny, nx, UNITS, TILE, LANES), F32),
-        pltpu.VMEM((nz, plane, cols), BF16),
+        pltpu.VMEM((nz, ny, nx, PARTS, BLOCK, LANES), F32),
+        pltpu.VMEM((nz, ny, nx, PARTS, BLOCK, LANES), BF16),
+        pltpu.VMEM((nz, ny, nx, PARTS, BLOCK, LANES), BF16),
         pltpu.VMEM((nz, plane, cols), BF16),
         pltpu.VMEM((4,) + vec_grads.shape[1:], F32),
         pltpu.VMEM((wires,) + vec_grads.shape[1:], F32),
@@ -466,15 +468,15 @@
         pltpu.VMEM((mats, rank, rows), F32),
         pltpu.VMEM((UNITS, BLOCK, LANES), BF16),
     ]
-    for order, _, count in ORDERS:
+    for order, (_, count), _ in ORDERS:
         first, second, third = order
         halved = 1 if first == 0 else 0
         shape = [sizes[a] // 2 if a == halved else sizes[a] for a in range(3) if a != first]
         hops = len(hop_table(sizes[first]))
-        tail = (count, TILE, LANES)
-        scratch.append(pltpu.VMEM((hops, *shape, *tail), F32))
-        scratch.append(pltpu.VMEM((sizes[second] - 1, sizes[third], *tail), F32))
-        scratch.append(pltpu.VMEM((sizes[third] - 1, *tail), F32))
+        tail = (count, BLOCK, LANES)
+        scratch.append(pltpu.VMEM((hops, *shape, *tail), BF16))
+        scratch.append(pltpu.VMEM((sizes[second] - 1, sizes[third], *tail), BF16))
+        scratch.append(pltpu.VMEM((sizes[third] - 1, *tail), BF16))
         counts = [hops, sizes[second] - 1, sizes[third] - 1]
         counts = counts + counts[::-1] + counts[::-1]
         for _ in range(2):
@@ -606,9 +608,10 @@
     local_block = jnp.sum(mine * index[None, :], axis=1)
     valid = jnp.sum(mine, axis=1)
     table = jnp.concatenate([lax.axis_index("sub").astype(jnp.int32)[None], pos, local_block, valid])
-    basis, right, vec, gathered = share(sizes, grads, errors, vec_grads, q_start, momentum, master)
+    basis, right, vec, gathered = share(
+        sizes, grads, errors, vec_grads, jnp.swapaxes(q_start, 1, 2), momentum, master
+    )
     gathered = gathered.reshape(replicas * slots, 2, BLOCK, LANES)
-    vec = vec * (VECTOR_RATE / replicas)
     errors_out, new_gains, new_momentum, new_master, weights = finish(
         sizes[0], table, grads, errors, basis, right, gathered, momentum, master, vec, gains
     )

time: 162 us -> 128 us (0.79)
  Pallas kernels: 154 us -> 124 us
  local copies, waits for them, and re-layouts: 1.9 us -> 0 us
    pallas_call x1, Pallas kernels: 145 us -> 114 us  [share(): pl.pallas_call(functools.partial(share_kernel, sizes), out_shape=(jax.Sha...]
    unnamed x1 -> x0, local copies, waits for them, and re-layouts: 1.9 us -> none
where the time goes in v2:
time: 128 us
  Pallas kernels  124 us (97%)
  other arithmetic  3.13 us (2%)
    pallas_call x1, Pallas kernels, share(): pl.pallas_call(functools.partial(share_kernel, sizes), out_shape=(jax.Sha...  114 us
    pallas_call x1, Pallas kernels, finish(): pl.pallas_call(functools.partial(finish_kernel, steps), grid_spec=pltpu.P...  9.93 us

profile of v2, /device:TPU:1, one launch (start us, length us, event | category | flops | bytes accessed | tf_op | source)
XLA Modules:
  0.0 127.8 jit_solution(8650606135933032351)
XLA Ops:
  0.6 0.7 broadcast_compare_fusion
  1.3 0.9 convert_reduce_fusion
  2.3 0.2 select_reduce_fusion
  2.4 0.7 multiply_add_fusion
  3.1 0.7 pad_add_fusion.table
  3.8 114.1 %share.1 = (f32[2,2,32,1024]{3,2,1,0:T(8,128)}, f32[2,32,512]{2,1,0:T(8,128)}, f32[2,1024]{1,0:T(2,128)}, bf16[8,4,4,8,16,128]{5,4,3,2,1,0:T(8,128)(2,1)}) custom-call(bf16[1,2,1024,512]{3,2,1,0:T(8,128)(2,1)} %grads.1, bf16[1,2,1024,512]{3,2,1,0:T(8,128)(2,1)} %errors.1, f32[1,2,1024]{2,1,0:T(2,128)} %refs_2_.1, f32[2,32,512]{2,1,0:T(8,128)} %bitcast.4, ...), custom_call_target="tpu_custom_call" | custom-call | tf_op jit(solution)/shard_map/share/pallas_call | solution.py:484
  117.8 9.9 %finish.1 = (bf16[1,2,1024,512]{3,2,1,0:T(8,128)(2,1)}, f32[2,1024]{1,0:T(2,128)}, f32[4,16,256]{2,1,0:T(8,128)}, f32[4,16,256]{2,1,0:T(8,128)}, bf16[2,2048,256]{2,1,0:T(8,128)(2,1)}) custom-call(s32[265]{0:T(512)} %pad_add_fusion.table, bf16[1,2,1024,512]{3,2,1,0:T(8,128)(2,1)} %grads.1, bf16[1,2,1024,512]{3,2,1,0:T(8,128)(2,1)} %errors.1, ...), custom_call_target="tpu_custom_call" | custom-call | tf_op jit(solution)/shard_map/finish/pallas_call | solution.py:559

commit v3 on v2

--- a/solution.py
+++ b/solution.py
@@ -20,7 +20,10 @@
 LANES = 128
 BLOCK = 16
 UNITS = 8
+STRIDE = 4
 PARTS = 4
+
+SLOT_ORDERS = ((2, 1, 0), (1, 2, 0), (0, 2, 1))
 
 ORDERS = (((2, 1, 0), (0, 2), (0, 3)), ((1, 0, 2), (2, 1), (3, 3)), ((0, 2, 1), (3, 1), (6, 2)))
 
@@ -72,15 +75,42 @@
     table = jnp.concatenate([gram0, eye, gram1, eye], axis=1)
     first = lanes < 2 * rank
     pivots = jnp.ones((rank, LANES), F32)
-    for k in range(rank):
-        column = jnp.where(first, table[:, k : k + 1], table[:, 2 * rank + k : 2 * rank + k + 1])
-        pivot = column[k : k + 1, :]
-        pivots = jnp.where(rows == k, pivot, pivots)
-        if k < rank - 1:
-            scaled = table[k : k + 1, :] / pivot
-            table = table - jnp.where(rows > k, column * scaled, 0.0)
+    for k in range(0, rank, STRIDE):
+        columns, lines = [], []
+        for j in range(k, k + STRIDE):
+            columns.append(jnp.where(first, table[:, j : j + 1], table[:, 2 * rank + j : 2 * rank + j + 1]))
+            lines.append(table[j : j + 1, :])
+        change = jnp.zeros((rank, LANES), F32)
+        for j in range(STRIDE):
+            pivot = columns[j][k + j : k + j + 1, :]
+            pivots = jnp.where(rows == k + j, pivot, pivots)
+            inverse = 1.0 / pivot
+            scaled = lines[j] * inverse
+            for i in range(j + 1, STRIDE):
+                factor = columns[j][k + i : k + i + 1, :]
+                lines[i] = lines[i] - factor * scaled
+                columns[i] = columns[i] - columns[j] * (factor * inverse)
+            change = change + jnp.where(rows > k + j, columns[j] * scaled, 0.0)
+        table = table - change
     table = table * lax.rsqrt(pivots)
     return table[:, rank : 2 * rank], table[:, 3 * rank : 4 * rank]
+
+
+def place_blocks(owner, dp, sub, slots):
+    blocks = owner.shape[1]
+    wide = jnp.broadcast_to(owner.astype(F32), (blocks, blocks))
+    before = lax.broadcasted_iota(jnp.int32, wide.shape, 0)
+    block = lax.broadcasted_iota(jnp.int32, wide.shape, 1)
+    rank = jnp.sum(jnp.where((wide == wide.T) & (before < block), 1.0, 0.0), axis=0, keepdims=True)
+    rank = rank.astype(jnp.int32)
+    lines = [owner * slots + rank]
+    for slot in range(slots):
+        held = jnp.where((owner == dp) & (rank == slot), block[:1] + 1, 0).astype(F32)
+        held = jnp.sum(held, axis=1, keepdims=True).astype(jnp.int32) - 1
+        lines.append(jnp.broadcast_to(held, (1, blocks)))
+    lines.append(jnp.broadcast_to(sub, (1, blocks)).astype(jnp.int32))
+    lines.append(jnp.zeros((8 - len(lines), blocks), jnp.int32))
+    return jnp.concatenate(lines, axis=0)
 
 
 class Exchange:
@@ -275,8 +305,8 @@
 def share_kernel(sizes, *refs):
     refs = list(refs)
     take = lambda count: [refs.pop(0) for _ in range(count)]
-    grads, errors, vec_grads, q_start, momentum, master = take(6)
-    basis_out, right_out, vec_out, slots_out = take(4)
+    grads, errors, vec_grads, q_start, momentum, master, owner = take(7)
+    basis_out, right_out, vec_out, slots_out, table_out = take(5)
     raw_g, raw_e, load_sem, work, wire, mean = take(6)
     high = take(1)[0]
     vec_buf, vec_land, vec_send, vec_recv = take(4)
@@ -354,14 +384,14 @@
         next(spreads[number])
 
     def early(number):
-        order, _, units = ORDERS[number]
+        order, units = SLOT_ORDERS[number], ORDERS[number][2]
         send, recv = sends[number], recvs[number]
         yield from direct_gather(ex, slots_out, send[6], recv[6], order, 2, units)
         yield from direct_gather(ex, slots_out, send[7], recv[7], order, 1, units)
         gathered[number] = True
 
     def spread(number):
-        order, _, units = ORDERS[number]
+        order, units = SLOT_ORDERS[number], ORDERS[number][2]
         yield from ring_gather(ex, slots_out, sends[number][8], recvs[number][8], order, units)
 
     spreads = [spread(number) for number in range(3)]
@@ -370,6 +400,7 @@
         vector_sum(ex, vec_buf, vec_land, vec_send, vec_recv),
         *[early(number) for number in range(3)],
     )
+    table_out[...] = place_blocks(owner[...], lax.axis_index("dp"), ex.sub, momentum.shape[0])
     vec_out[...] = vec_buf[3] * (VECTOR_RATE / dp_count)
 
     def advance():
@@ -438,7 +469,7 @@
         made.wait_send()
 
 
-def share(sizes, grads, errors, vec_grads, q_start, momentum, master):
+def share(sizes, grads, errors, vec_grads, q_start, momentum, master, owner):
     nz, ny, nx = sizes
     mats, rows, cols = grads.shape[1:]
     rank = q_start.shape[1]
@@ -468,7 +499,7 @@
         pltpu.VMEM((mats, rank, rows), F32),
         pltpu.VMEM((UNITS, BLOCK, LANES), BF16),
     ]
-    for order, (_, count), _ in ORDERS:
+    for (order, (_, count), _), slot_order in zip(ORDERS, SLOT_ORDERS):
         first, second, third = order
         halved = 1 if first == 0 else 0
         shape = [sizes[a] // 2 if a == halved else sizes[a] for a in range(3) if a != first]
@@ -478,7 +509,7 @@
         scratch.append(pltpu.VMEM((sizes[second] - 1, sizes[third], *tail), BF16))
         scratch.append(pltpu.VMEM((sizes[third] - 1, *tail), BF16))
         counts = [hops, sizes[second] - 1, sizes[third] - 1]
-        counts = counts + counts[::-1] + counts[::-1]
+        counts = counts + counts[::-1] + [sizes[slot_order[2]] - 1, sizes[slot_order[1]] - 1, hops]
         for _ in range(2):
             scratch.extend(dma((n,)) for n in counts)
     return pl.pallas_call(
@@ -488,23 +519,23 @@
             jax.ShapeDtypeStruct((mats, rank, cols), F32),
             jax.ShapeDtypeStruct(vec_grads.shape[1:], F32),
             jax.ShapeDtypeStruct((nz, ny, nx, UNITS, BLOCK, LANES), BF16),
+            jax.ShapeDtypeStruct((8, owner.shape[1]), jnp.int32),
         ),
-        in_specs=[anywhere, anywhere, vmem, vmem, vmem, vmem],
-        out_specs=(vmem, vmem, vmem, anywhere),
+        in_specs=[anywhere, anywhere, vmem, vmem, vmem, vmem, vmem],
+        out_specs=(vmem, vmem, vmem, anywhere, vmem),
         scratch_shapes=scratch,
         compiler_params=pltpu.CompilerParams(
             collective_id=0, has_side_effects=True, vmem_limit_bytes=56 * 1024 * 1024
         ),
         name="share",
-    )(grads, errors, vec_grads, q_start, momentum, master)
+    )(grads, errors, vec_grads, q_start, momentum, master, owner)
 
 
 def finish_kernel(steps, table, grads, errors, basis, right, gathered, momentum, master, vec, gains, *rest):
     errors_out, new_gains, new_momentum, new_master, weights, approx = rest
     step = pl.program_id(0)
-    sub = table[0]
-    blocks = approx.shape[0]
     slots = momentum.shape[0]
+    sub = table[1 + slots, 0]
     per_mat = steps // 2
     mat = step // per_mat
     part = lax.rem(step, per_mat)
@@ -531,7 +562,7 @@
 
     for number in range(per_step):
         block = step * per_step + number
-        at = table[1 + block]
+        at = table[0, block]
         for group in range(half_cols // LANES):
             lanes = slice(group * LANES, (group + 1) * LANES)
             value = gathered[at, group].astype(F32) - STEP_RATE * approx[block, :, lanes]
@@ -541,8 +572,9 @@
     def _():
         new_gains[...] = gains[...] - vec[...]
         for slot in range(slots):
-            valid = table[1 + blocks + slots + slot] > 0
-            moved = MOMENTUM_DECAY * momentum[slot] + approx[table[1 + blocks + slot]]
+            block = table[1 + slot, 0]
+            valid = block >= 0
+            moved = MOMENTUM_DECAY * momentum[slot] + approx[jnp.maximum(block, 0)]
             moved = jnp.where(valid, moved, 0.0)
             new_momentum[slot] = moved
             new_master[slot] = jnp.where(valid, master[slot] - STEP_RATE * moved, 0.0)
@@ -597,19 +629,8 @@
     replicas = lax.axis_size("dp")
     sizes = torus(replicas)
     slots = momentum.shape[0]
-    blocks = owner.shape[0]
-    index = jnp.arange(blocks, dtype=jnp.int32)
-    same = owner[:, None] == owner[None, :]
-    earlier = index[None, :] < index[:, None]
-    rank = jnp.sum((same & earlier).astype(jnp.int32), axis=1)
-    pos = owner * slots + rank
-    mine = (owner[None, :] == lax.axis_index("dp")) & (rank[None, :] == jnp.arange(slots, dtype=jnp.int32)[:, None])
-    mine = mine.astype(jnp.int32)
-    local_block = jnp.sum(mine * index[None, :], axis=1)
-    valid = jnp.sum(mine, axis=1)
-    table = jnp.concatenate([lax.axis_index("sub").astype(jnp.int32)[None], pos, local_block, valid])
-    basis, right, vec, gathered = share(
-        sizes, grads, errors, vec_grads, jnp.swapaxes(q_start, 1, 2), momentum, master
+    basis, right, vec, gathered, table = share(
+        sizes, grads, errors, vec_grads, jnp.swapaxes(q_start, 1, 2), momentum, master, owner[None]
     )
     gathered = gathered.reshape(replicas * slots, 2, BLOCK, LANES)
     errors_out, new_gains, new_momentum, new_master, weights = finish(

time: 128 us -> 120 us (0.938)
  Pallas kernels: 124 us -> 119 us
  other arithmetic: 3.13 us -> 0 us
    pallas_call x1, Pallas kernels: 114 us -> 109 us  [share(): pl.pallas_call(functools.partial(share_kernel, sizes), out_shape=(jax.Sha...]
where the time goes in v3:
time: 120 us
  Pallas kernels  119 us (99%)
    pallas_call x1, Pallas kernels, share(): pl.pallas_call(functools.partial(share_kernel, sizes), out_shape=(jax.Sha...  109 us
    pallas_call x1, Pallas kernels, finish(): pl.pallas_call(functools.partial(finish_kernel, steps), grid_spec=pltpu.P...  10 us

profile of v3, /device:TPU:1, one launch (start us, length us, event | category | flops | bytes accessed | tf_op | source)
XLA Modules:
  0.0 119.6 jit_solution(17525409525080401270)
XLA Ops:
  0.6 108.9 %share.1 = (f32[2,2,32,1024]{3,2,1,0:T(8,128)}, f32[2,32,512]{2,1,0:T(8,128)}, f32[2,1024]{1,0:T(2,128)}, bf16[8,4,4,8,16,128]{5,4,3,2,1,0:T(8,128)(2,1)}, s32[8,256]{1,0:T(8,128)}) custom-call(bf16[1,2,1024,512]{3,2,1,0:T(8,128)(2,1)} %grads.1, bf16[1,2,1024,512]{3,2,1,0:T(8,128)(2,1)} %errors.1, f32[1,2,1024]{2,1,0:T(2,128)} %refs_2_.1, ...), custom_call_target="tpu_custom_call" | custom-call | tf_op jit(solution)/shard_map/share/pallas_call | solution.py:515
  109.5 10.0 %finish.1 = (bf16[1,2,1024,512]{3,2,1,0:T(8,128)(2,1)}, f32[2,1024]{1,0:T(2,128)}, f32[4,16,256]{2,1,0:T(8,128)}, f32[4,16,256]{2,1,0:T(8,128)}, bf16[2,2048,256]{2,1,0:T(8,128)(2,1)}) custom-call(s32[8,256]{1,0:T(8,128)} %get-tuple-element.10.table, bf16[1,2,1024,512]{3,2,1,0:T(8,128)(2,1)} %grads.1, bf16[1,2,1024,512]{3,2,1,0:T(8,128)(2,1)} %errors.1, ...), custom_call_target="tpu_custom_call" | custom-call | tf_op jit(solution)/shard_map/finish/pallas_call | solution.py:591

commit v4 on v3

--- a/solution.py
+++ b/solution.py
@@ -20,7 +20,7 @@
 LANES = 128
 BLOCK = 16
 UNITS = 8
-STRIDE = 4
+STRIDE = 8
 PARTS = 4
 
 SLOT_ORDERS = ((2, 1, 0), (1, 2, 0), (0, 2, 1))
@@ -394,13 +394,17 @@
         order, units = SLOT_ORDERS[number], ORDERS[number][2]
         yield from ring_gather(ex, slots_out, sends[number][8], recvs[number][8], order, units)
 
+    def tabulate():
+        yield
+        table_out[...] = place_blocks(owner[...], lax.axis_index("dp"), ex.sub, momentum.shape[0])
+
     spreads = [spread(number) for number in range(3)]
     interleave(
         *[scatter(number) for number in range(3)],
         vector_sum(ex, vec_buf, vec_land, vec_send, vec_recv),
         *[early(number) for number in range(3)],
+        tabulate(),
     )
-    table_out[...] = place_blocks(owner[...], lax.axis_index("dp"), ex.sub, momentum.shape[0])
     vec_out[...] = vec_buf[3] * (VECTOR_RATE / dp_count)
 
     def advance():

time: 120 us -> 120 us (level)
  no operation moved by 1% of the time
where the time goes in v4:
time: 120 us; the launch traced here: 119 us
  Pallas kernels  119 us (99%)
    pallas_call x1, Pallas kernels, share(): pl.pallas_call(functools.partial(share_kernel, sizes), out_shape=(jax.Sha...  109 us
    pallas_call x1, Pallas kernels, finish(): pl.pallas_call(functools.partial(finish_kernel, steps), grid_spec=pltpu.P...  10 us

profile of v4, /device:TPU:1, one launch (start us, length us, event | category | flops | bytes accessed | tf_op | source)
XLA Modules:
  0.0 119.5 jit_solution(4375134015413376160)
XLA Ops:
  0.6 108.8 %share.1 = (f32[2,2,32,1024]{3,2,1,0:T(8,128)}, f32[2,32,512]{2,1,0:T(8,128)}, f32[2,1024]{1,0:T(2,128)}, bf16[8,4,4,8,16,128]{5,4,3,2,1,0:T(8,128)(2,1)}, s32[8,256]{1,0:T(8,128)}) custom-call(bf16[1,2,1024,512]{3,2,1,0:T(8,128)(2,1)} %grads.1, bf16[1,2,1024,512]{3,2,1,0:T(8,128)(2,1)} %errors.1, f32[1,2,1024]{2,1,0:T(2,128)} %refs_2_.1, ...), custom_call_target="tpu_custom_call" | custom-call | tf_op jit(solution)/shard_map/share/pallas_call | solution.py:519
  109.4 10.0 %finish.1 = (bf16[1,2,1024,512]{3,2,1,0:T(8,128)(2,1)}, f32[2,1024]{1,0:T(2,128)}, f32[4,16,256]{2,1,0:T(8,128)}, f32[4,16,256]{2,1,0:T(8,128)}, bf16[2,2048,256]{2,1,0:T(8,128)(2,1)}) custom-call(s32[8,256]{1,0:T(8,128)} %get-tuple-element.10.table, bf16[1,2,1024,512]{3,2,1,0:T(8,128)(2,1)} %grads.1, bf16[1,2,1024,512]{3,2,1,0:T(8,128)(2,1)} %errors.1, ...), custom_call_target="tpu_custom_call" | custom-call | tf_op jit(solution)/shard_map/finish/pallas_call | solution.py:595
